TPU v7x, 512 devices: a whole 4x8x8 slice. The times are simulated.
512 devices in a mesh: seq: 128 (over x, y_hi, z, core), tp: 4 (over y_lo).
Axes of the slice: x: 4, y: 8 (y_hi: 2, y_lo: 4; y = y_hi * 4 + y_lo), z: 8, core: 2. Of those that a mesh axis runs over, the one named last changes fastest.
Arguments:
- tokens: bfloat16 [16384, 2560], P('seq', 'tp'), may hold values from -6 to 6
- seg_ids: int32 [16384], P('seq'), may hold values from 0 to 31, never falling along the last dimension, each value on 1 to 4096 neighbouring positions
- norm_gain: bfloat16 [2560], replicated, may hold values from 0.099609375 to 1.8984375
- w_query: bfloat16 [2560, 2048], P('seq', 'tp'), may hold values from -3 to 3
- w_keyval: bfloat16 [2560, 512], P('seq'), may hold values from -1 to 1
- w_out: bfloat16 [2048, 2560], P('tp', 'seq'), may hold values from -0.125 to 0.125
Outputs:
- hidden: bfloat16 [16384, 2560], P('seq', 'tp')
- kv_cache: bfloat16 [16384, 512], P('seq')
Inputs may be any that keep to these rules, and one draw needn't show every extreme that they name: `seg_ids`: ids never fall along the stream; each of the 32 requests holds 1 to 4096 consecutive tokens, one exactly 4096.
All inputs are finite; a program needn't handle non-finite values.
Results may differ from a plain program's by a relative error of at most 0.0085.
Values may be sent and summed in bfloat16 or wider, within the bound.
No kernel may reach another device: no remote copies, remote signals or barrier semaphores. Data moves between devices by JAX's collectives and lax.ppermute only.
A program may use at most 64 MiB of HBM per device.

v0:
```python
import jax
import jax.numpy as jnp
from jax import lax
from jax.sharding import PartitionSpec as P

HD = 256
WINDOW = 2048
SEG_MEAN = 512


def from_behind(x, axis, by):
    devices = lax.axis_size(axis)
    pairs = [(i, i + by) for i in range(devices) if 0 <= i + by < devices]
    return lax.ppermute(x, axis, pairs)


def rms_norm(values, gain):
    wide = values.astype(jnp.float32)
    scaled = wide * lax.rsqrt(jnp.mean(wide * wide, axis=-1, keepdims=True) + 1e-06)
    return (scaled * gain.astype(jnp.float32)).astype(jnp.bfloat16)


def rotate(tensor, positions):
    quarter = tensor.shape[-1] // 4
    freq = 10000.0 ** (-jnp.arange(quarter, dtype=jnp.float32) / quarter)
    angle = positions[:, None, None] * freq
    cosine = jnp.cos(angle)
    sine = jnp.sin(angle)
    first = tensor[..., :quarter]
    second = tensor[..., quarter : 2 * quarter]
    return jnp.concatenate(
        [
            first * cosine - second * sine,
            second * cosine + first * sine,
            tensor[..., 2 * quarter :],
        ],
        axis=-1,
    )


def per_device(tokens, seg_ids, norm_gain, w_query, w_keyval, w_out):
    tok_rows = tokens.shape[0]
    seq_count = lax.axis_size("seq")
    my_index = lax.axis_index("seq")
    gathered = lax.all_gather(tokens, "tp", axis=1, tiled=True)
    normed = rms_norm(gathered, norm_gain)
    seg_total = tok_rows * seq_count // SEG_MEAN
    labels = jnp.arange(seg_total, dtype=jnp.int32)
    below = jnp.sum((seg_ids[None, :] < labels[:, None]).astype(jnp.int32), axis=1)
    starts = lax.psum(below, "seq")
    own_start = jnp.sum(jnp.where(seg_ids[:, None] == labels[None, :], starts[None, :], 0), axis=1)
    token_index = my_index * tok_rows + jnp.arange(tok_rows, dtype=jnp.int32)
    positions = (token_index - own_start).astype(jnp.float32)
    query_raw = jnp.dot(
        normed,
        lax.all_gather(w_query, "seq", axis=0, tiled=True),
        preferred_element_type=jnp.float32,
    )
    keyval_raw = jnp.dot(
        normed,
        lax.all_gather(w_keyval, "seq", axis=0, tiled=True),
        preferred_element_type=jnp.float32,
    )
    local_heads = w_query.shape[1] // HD
    queries = rotate(query_raw.reshape(tok_rows, local_heads, HD), positions).astype(jnp.bfloat16)
    key_rows = rotate(keyval_raw[:, None, :HD], positions)[:, 0, :]
    kv_cache = jnp.concatenate([key_rows, keyval_raw[:, HD:]], axis=1).astype(jnp.bfloat16)
    reach = min(WINDOW // tok_rows, seq_count - 1)

    def advance(counter, state):
        current, current_seg, store, store_seg = state
        current, current_seg = from_behind((current, current_seg), "seq", 1)
        slot = reach - 1 - counter
        store = lax.dynamic_update_slice_in_dim(store, current[None], slot, 0)
        store_seg = lax.dynamic_update_slice_in_dim(store_seg, current_seg[None], slot, 0)
        return (current, current_seg, store, store_seg)

    store_init = jnp.zeros((reach, tok_rows, kv_cache.shape[1]), jnp.bfloat16)
    seg_init = jnp.zeros((reach, tok_rows), jnp.int32)
    final_state = lax.fori_loop(0, reach, advance, (kv_cache, seg_ids, store_init, seg_init))
    block_kv = jnp.concatenate(
        [final_state[2].reshape(reach * tok_rows, kv_cache.shape[1]), kv_cache], axis=0
    )
    block_seg = jnp.concatenate([final_state[3].reshape(reach * tok_rows), seg_ids], axis=0)
    key_index = (my_index - reach) * tok_rows + jnp.arange((reach + 1) * tok_rows, dtype=jnp.int32)
    live = (block_seg[None, :] == seg_ids[:, None]) & (key_index[None, :] <= token_index[:, None])
    live = live & (token_index[:, None] - key_index[None, :] < WINDOW) & (key_index[None, :] >= 0)
    all_keys = block_kv[:, :HD]
    all_values = block_kv[:, HD:]
    head_outputs = []
    for head_idx in range(local_heads):
        scores = lax.dot_general(
            queries[:, head_idx, :],
            all_keys,
            (((1,), (1,)), ((), ())),
            preferred_element_type=jnp.float32,
        ) * HD ** (-0.5)
        scores = jnp.where(live, scores, -1e30)
        peak = jnp.max(scores, axis=1, keepdims=True)
        powered = jnp.exp(scores - peak)
        weights = (powered / jnp.sum(powered, axis=1, keepdims=True)).astype(jnp.bfloat16)
        head_outputs.append(
            jnp.dot(weights, all_values, preferred_element_type=jnp.float32).astype(jnp.bfloat16)
        )
    attended = jnp.concatenate(head_outputs, axis=1)
    partial_value = jnp.dot(
        attended,
        lax.all_gather(w_out, "seq", axis=1, tiled=True),
        preferred_element_type=jnp.float32,
    )
    summed = lax.psum_scatter(
        partial_value.astype(jnp.bfloat16), "tp", scatter_dimension=1, tiled=True
    ).astype(jnp.float32)
    hidden = (tokens.astype(jnp.float32) + summed).astype(jnp.bfloat16)
    return (hidden, kv_cache)


def solution(mesh):
    in_specs = (P("seq", "tp"), P("seq"), P(), P("seq", "tp"), P("seq", None), P("tp", "seq"))
    out_specs = (P("seq", "tp"), P("seq", None))
    return jax.shard_map(
        per_device, mesh=mesh, in_specs=in_specs, out_specs=out_specs, check_vma=False
    )
```

profile of v0, /device:TPU:2, one launch (start us, length us, event | category | flops | bytes accessed | tf_op | source)
XLA Modules:
  0.0 562.5 jit_solution(2328956909194726290)
XLA Ops:
  10.2 18.5 %all_gather.12 = bf16[128,2560]{1,0:T(8,128)(2,1)S(1)} all-gather(bf16[128,640]{1,0:T(8,128)(2,1)} %param.8), channel_id=1, replica_groups=mesh['seq'=128,'tp'=4] {'tp'}, dimensions={1}, use_global_device_ids=true | all-gather | bytes 819200 | tf_op jit(solution)/shard_map/all_gather | solution.py:45
  28.9 31.9 %psum.7 = s32[32]{0:T(128)S(1)} all-reduce(s32[32]{0:T(128)S(1)} %convert_reduce_fusion), channel_id=1, replica_groups=mesh['seq'=128,'tp'=4] {'seq'}, use_global_device_ids=true, to_apply=%region_2.0 | all-reduce | flops 32 | bytes 256 | tf_op jit(solution)/shard_map/psum | solution.py:50
  61.5 1.0 multiply_cosine_fusion
  62.4 85.6 %all-gather.7.cloned.1.call-done = bf16[128,20,512]{2,1,0:T(8,128)(2,1)} async-done(((bf16[1,20,512]{2,1,0:T(8,128)(2,1)}), bf16[128,20,512]{2,1,0:T(8,128)(2,1)}) %all-gather.7.cloned.1.call-update) | async-done | bytes 2621456 | tf_op jit(solution)/shard_map/all_gather | solution.py:61
  148.0 3.6 reshape.164
  151.6 1.2 fusion.16
  154.9 125.2 %all-gather.9.cloned.1.call-done = bf16[128,20,512]{2,1,0:T(8,128)(2,1)} async-done(((bf16[1,20,512]{2,1,0:T(8,128)(2,1)}), bf16[128,20,512]{2,1,0:T(8,128)(2,1)}) %all-gather.9.cloned.1.call-update) | async-done | bytes 2621456 | tf_op jit(solution)/shard_map/all_gather | solution.py:56
  280.1 3.6 reshape.166
  283.7 1.2 fusion.14
  286.0 0.8 pad_maximum_fusion.3
  287.7 223.8 %while.19 = (s32[]{:T(128)}, bf16[128,512]{1,0:T(8,128)(2,1)S(1)}, s32[128]{0:T(128)S(1)}, bf16[16,128,512]{2,1,0:T(8,128)(2,1)S(1)}, s32[16,128]{1,0:T(8,128)S(...) while((s32[]{:T(128)}, bf16[128,512]{1,0:T(8,128)(2,1)S(1)}, s32[128]{0:T(128)S(1)}, ...), condition=%wide.region_5.6_spmd, body=%wide.region_4.5_spmd.sunk | while | flops 6 | bytes 1052899 | solution.py:80
  287.7 2.3 collective-permute-start
  289.9 2.4 collective-permute-start.1
  292.3 9.4 %collective-permute-done.1 = s32[128]{0:T(128)S(1)} collective-permute-done((s32[128]{0:T(128)S(1)}, s32[128]{0:T(128)S(1)}, u32[]{:S(2)}, u32[]{:S(2)}) %collective-permute-start.1) | collective-permute-done | bytes 544 | tf_op jit(solution)/shard_map/while/body/eval_jaxpr/ppermute | solution.py:14
  301.8 1.9 collective-permute-start
  303.8 1.9 collective-permute-start.1
  305.7 9.9 %collective-permute-done.1 = s32[128]{0:T(128)S(1)} collective-permute-done((s32[128]{0:T(128)S(1)}, s32[128]{0:T(128)S(1)}, u32[]{:S(2)}, u32[]{:S(2)}) %collective-permute-start.1) | collective-permute-done | bytes 544 | tf_op jit(solution)/shard_map/while/body/eval_jaxpr/ppermute | solution.py:14
  315.7 1.9 collective-permute-start
  317.6 1.9 collective-permute-start.1
  319.6 10.9 %collective-permute-done.1 = s32[128]{0:T(128)S(1)} collective-permute-done((s32[128]{0:T(128)S(1)}, s32[128]{0:T(128)S(1)}, u32[]{:S(2)}, u32[]{:S(2)}) %collective-permute-start.1) | collective-permute-done | bytes 544 | tf_op jit(solution)/shard_map/while/body/eval_jaxpr/ppermute | solution.py:14
  330.6 1.9 collective-permute-start
  332.5 1.9 collective-permute-start.1
  334.5 9.9 %collective-permute-done.1 = s32[128]{0:T(128)S(1)} collective-permute-done((s32[128]{0:T(128)S(1)}, s32[128]{0:T(128)S(1)}, u32[]{:S(2)}, u32[]{:S(2)}) %collective-permute-start.1) | collective-permute-done | bytes 544 | tf_op jit(solution)/shard_map/while/body/eval_jaxpr/ppermute | solution.py:14
  344.4 1.9 collective-permute-start
  346.4 1.9 collective-permute-start.1
  348.3 9.9 %collective-permute-done.1 = s32[128]{0:T(128)S(1)} collective-permute-done((s32[128]{0:T(128)S(1)}, s32[128]{0:T(128)S(1)}, u32[]{:S(2)}, u32[]{:S(2)}) %collective-permute-start.1) | collective-permute-done | bytes 544 | tf_op jit(solution)/shard_map/while/body/eval_jaxpr/ppermute | solution.py:14
  358.3 1.9 collective-permute-start
  360.2 1.9 collective-permute-start.1
  362.1 9.9 %collective-permute-done.1 = s32[128]{0:T(128)S(1)} collective-permute-done((s32[128]{0:T(128)S(1)}, s32[128]{0:T(128)S(1)}, u32[]{:S(2)}, u32[]{:S(2)}) %collective-permute-start.1) | collective-permute-done | bytes 544 | tf_op jit(solution)/shard_map/while/body/eval_jaxpr/ppermute | solution.py:14
  372.1 1.9 collective-permute-start
  374.0 1.9 collective-permute-start.1
  375.9 9.9 %collective-permute-done.1 = s32[128]{0:T(128)S(1)} collective-permute-done((s32[128]{0:T(128)S(1)}, s32[128]{0:T(128)S(1)}, u32[]{:S(2)}, u32[]{:S(2)}) %collective-permute-start.1) | collective-permute-done | bytes 544 | tf_op jit(solution)/shard_map/while/body/eval_jaxpr/ppermute | solution.py:14
  386.0 1.9 collective-permute-start
  387.9 1.9 collective-permute-start.1
  389.8 11.0 %collective-permute-done.1 = s32[128]{0:T(128)S(1)} collective-permute-done((s32[128]{0:T(128)S(1)}, s32[128]{0:T(128)S(1)}, u32[]{:S(2)}, u32[]{:S(2)}) %collective-permute-start.1) | collective-permute-done | bytes 544 | tf_op jit(solution)/shard_map/while/body/eval_jaxpr/ppermute | solution.py:14
  400.9 1.9 collective-permute-start
  402.8 1.9 collective-permute-start.1
  404.8 9.9 %collective-permute-done.1 = s32[128]{0:T(128)S(1)} collective-permute-done((s32[128]{0:T(128)S(1)}, s32[128]{0:T(128)S(1)}, u32[]{:S(2)}, u32[]{:S(2)}) %collective-permute-start.1) | collective-permute-done | bytes 544 | tf_op jit(solution)/shard_map/while/body/eval_jaxpr/ppermute | solution.py:14
  414.7 1.9 collective-permute-start
  416.7 1.9 collective-permute-start.1
  418.6 9.9 %collective-permute-done.1 = s32[128]{0:T(128)S(1)} collective-permute-done((s32[128]{0:T(128)S(1)}, s32[128]{0:T(128)S(1)}, u32[]{:S(2)}, u32[]{:S(2)}) %collective-permute-start.1) | collective-permute-done | bytes 544 | tf_op jit(solution)/shard_map/while/body/eval_jaxpr/ppermute | solution.py:14
  428.6 1.9 collective-permute-start
  430.5 1.9 collective-permute-start.1
  432.4 9.9 %collective-permute-done.1 = s32[128]{0:T(128)S(1)} collective-permute-done((s32[128]{0:T(128)S(1)}, s32[128]{0:T(128)S(1)}, u32[]{:S(2)}, u32[]{:S(2)}) %collective-permute-start.1) | collective-permute-done | bytes 544 | tf_op jit(solution)/shard_map/while/body/eval_jaxpr/ppermute | solution.py:14
  442.4 1.9 collective-permute-start
  444.3 1.9 collective-permute-start.1
  446.2 9.9 %collective-permute-done.1 = s32[128]{0:T(128)S(1)} collective-permute-done((s32[128]{0:T(128)S(1)}, s32[128]{0:T(128)S(1)}, u32[]{:S(2)}, u32[]{:S(2)}) %collective-permute-start.1) | collective-permute-done | bytes 544 | tf_op jit(solution)/shard_map/while/body/eval_jaxpr/ppermute | solution.py:14
  456.2 1.9 collective-permute-start
  458.1 1.9 collective-permute-start.1
  460.1 9.9 %collective-permute-done.1 = s32[128]{0:T(128)S(1)} collective-permute-done((s32[128]{0:T(128)S(1)}, s32[128]{0:T(128)S(1)}, u32[]{:S(2)}, u32[]{:S(2)}) %collective-permute-start.1) | collective-permute-done | bytes 544 | tf_op jit(solution)/shard_map/while/body/eval_jaxpr/ppermute | solution.py:14
  470.0 1.9 collective-permute-start
  472.0 1.9 collective-permute-start.1
  473.9 9.9 %collective-permute-done.1 = s32[128]{0:T(128)S(1)} collective-permute-done((s32[128]{0:T(128)S(1)}, s32[128]{0:T(128)S(1)}, u32[]{:S(2)}, u32[]{:S(2)}) %collective-permute-start.1) | collective-permute-done | bytes 544 | tf_op jit(solution)/shard_map/while/body/eval_jaxpr/ppermute | solution.py:14
  483.9 1.9 collective-permute-start
  485.8 1.9 collective-permute-start.1
  487.7 9.9 %collective-permute-done.1 = s32[128]{0:T(128)S(1)} collective-permute-done((s32[128]{0:T(128)S(1)}, s32[128]{0:T(128)S(1)}, u32[]{:S(2)}, u32[]{:S(2)}) %collective-permute-start.1) | collective-permute-done | bytes 544 | tf_op jit(solution)/shard_map/while/body/eval_jaxpr/ppermute | solution.py:14
  497.7 1.9 collective-permute-start
  499.6 1.9 collective-permute-start.1
  501.5 9.9 %collective-permute-done.1 = s32[128]{0:T(128)S(1)} collective-permute-done((s32[128]{0:T(128)S(1)}, s32[128]{0:T(128)S(1)}, u32[]{:S(2)}, u32[]{:S(2)}) %collective-permute-start.1) | collective-permute-done | bytes 544 | tf_op jit(solution)/shard_map/while/body/eval_jaxpr/ppermute | solution.py:14
  515.1 3.6 reshape.168
  518.8 1.0 convolution_convert_fusion
  519.7 1.1 copy.26
  520.9 33.3 %reduce-scatter.4.cloned.1.call-done = bf16[640,128]{1,0:T(8,128)(2,1)} async-done(((bf16[2560,128]{1,0:T(8,128)(2,1)}), bf16[640,128]{1,0:T(8,128)(2,1)}) %reduce-scatter.4.cloned.1.call-update) | async-done | bytes 163856
  554.2 1.1 copy.27
  (141 shorter events, 12.9 us)
Async XLA Ops:
  7.2 53.7 %copy-start.6 = (s32[128]{0:T(128)S(1)}, s32[128]{0:T(128)}, u32[]{:S(2)}) copy-start(s32[128]{0:T(128)} %param.9) | copy-start | bytes 1540
  7.2 21.7 %copy-start.4 = (bf16[2560]{0:T(1024)(128)(2,1)S(1)}, bf16[2560]{0:T(1024)(128)(2,1)}, u32[]{:S(2)}) copy-start(bf16[2560]{0:T(1024)(128)(2,1)} %param.10) | copy-start | bytes 15364
  7.2 140.8 %all-gather.7.cloned.1.call-start = ((), (), s32[]{:S(2)}) async-start(), calls=%async_computation.1 | async-start | bytes 3170304 | tf_op jit(solution)/shard_map/all_gather | solution.py:61
  7.9 272.1 %all-gather.9.cloned.1.call-start = ((), (), s32[]{:S(2)}) async-start(), calls=%async_computation.2 | async-start | bytes 3170304 | tf_op jit(solution)/shard_map/all_gather | solution.py:56
  8.7 506.4 %all-gather.11.cloned.1.call-start = ((), (), s32[]{:S(2)}) async-start(), calls=%async_computation.3 | async-start | bytes 3170304 | tf_op jit(solution)/shard_map/all_gather | solution.py:108
  9.4 544.8 %reduce-scatter.4.cloned.1.call-start = ((), (), s32[]{:S(2)}) async-start(), calls=%async_computation.4 | async-start | bytes 819200
  28.9 122.7 %copy-start.5 = (f32[128]{0:T(128)}, f32[128]{0:T(128)S(1)}, u32[]{:S(2)}) copy-start(f32[128]{0:T(128)S(1)} %add_rsqrt_fusion) | copy-start | bytes 1540
  286.9 227.7 %copy-start.1 = (bf16[128,512]{1,0:T(8,128)(2,1)}, bf16[128,512]{1,0:T(8,128)(2,1)S(1)}, u32[]{:S(2)}) copy-start(bf16[128,512]{1,0:T(8,128)(2,1)S(1)} %copy.19) | copy-start | bytes 393220
  287.0 0.7 copy-start.8
  287.7 223.9 %copy-start.7 = (s32[128]{0:T(128)S(1)}, s32[128]{0:T(128)}, u32[]{:S(2)}) copy-start(s32[128]{0:T(128)} %param.9) | copy-start | bytes 1540
  287.7 224.1 %copy-start.2 = (f32[128,64]{1,0:T(8,128)S(1)}, f32[128,64]{1,0:T(8,128)}, u32[]{:S(2)}) copy-start(f32[128,64]{1,0:T(8,128)} %get-tuple-element.122) | copy-start | bytes 98308
  287.7 224.1 %copy-start.3 = (f32[128,64]{1,0:T(8,128)S(1)}, f32[128,64]{1,0:T(8,128)}, u32[]{:S(2)}) copy-start(f32[128,64]{1,0:T(8,128)} %get-tuple-element.123) | copy-start | bytes 98308
  287.7 14.1 %collective-permute-start = (bf16[128,512]{1,0:T(8,128)(2,1)S(1)}, bf16[128,512]{1,0:T(8,128)(2,1)S(1)}, u32[]{:S(2)}, u32[]{:S(2)}) collective-permute-start(bf16[128,512]{1,0:T(8,128)(2,1)S(1)} %get-tuple-element.171), channel_id=1, source_target_pairs={{0,4},{4,8},{8,12},{12,16},{16,20},{20,24},{24,28},{28,32},{32,36}... | collective-permute-start | bytes 393224 | tf_op jit(solution)/shard_map/while/body/eval_jaxpr/ppermute | solution.py:14
  289.9 11.8 %collective-permute-start.1 = (s32[128]{0:T(128)S(1)}, s32[128]{0:T(128)S(1)}, u32[]{:S(2)}, u32[]{:S(2)}) collective-permute-start(s32[128]{0:T(128)S(1)} %get-tuple-element.172), channel_id=1, source_target_pairs={{0,4},{4,8},{8,12},{12,16},{16,20},{20,24},{24,28},{28,32},{32,36}... | collective-permute-start | bytes 1544 | tf_op jit(solution)/shard_map/while/body/eval_jaxpr/ppermute | solution.py:14
  301.8 13.8 %collective-permute-start = (bf16[128,512]{1,0:T(8,128)(2,1)S(1)}, bf16[128,512]{1,0:T(8,128)(2,1)S(1)}, u32[]{:S(2)}, u32[]{:S(2)}) collective-permute-start(bf16[128,512]{1,0:T(8,128)(2,1)S(1)} %get-tuple-element.171), channel_id=1, source_target_pairs={{0,4},{4,8},{8,12},{12,16},{16,20},{20,24},{24,28},{28,32},{32,36}... | collective-permute-start | bytes 393224 | tf_op jit(solution)/shard_map/while/body/eval_jaxpr/ppermute | solution.py:14
  303.8 11.9 %collective-permute-start.1 = (s32[128]{0:T(128)S(1)}, s32[128]{0:T(128)S(1)}, u32[]{:S(2)}, u32[]{:S(2)}) collective-permute-start(s32[128]{0:T(128)S(1)} %get-tuple-element.172), channel_id=1, source_target_pairs={{0,4},{4,8},{8,12},{12,16},{16,20},{20,24},{24,28},{28,32},{32,36}... | collective-permute-start | bytes 1544 | tf_op jit(solution)/shard_map/while/body/eval_jaxpr/ppermute | solution.py:14
  315.7 14.8 %collective-permute-start = (bf16[128,512]{1,0:T(8,128)(2,1)S(1)}, bf16[128,512]{1,0:T(8,128)(2,1)S(1)}, u32[]{:S(2)}, u32[]{:S(2)}) collective-permute-start(bf16[128,512]{1,0:T(8,128)(2,1)S(1)} %get-tuple-element.171), channel_id=1, source_target_pairs={{0,4},{4,8},{8,12},{12,16},{16,20},{20,24},{24,28},{28,32},{32,36}... | collective-permute-start | bytes 393224 | tf_op jit(solution)/shard_map/while/body/eval_jaxpr/ppermute | solution.py:14
  317.6 12.9 %collective-permute-start.1 = (s32[128]{0:T(128)S(1)}, s32[128]{0:T(128)S(1)}, u32[]{:S(2)}, u32[]{:S(2)}) collective-permute-start(s32[128]{0:T(128)S(1)} %get-tuple-element.172), channel_id=1, source_target_pairs={{0,4},{4,8},{8,12},{12,16},{16,20},{20,24},{24,28},{28,32},{32,36}... | collective-permute-start | bytes 1544 | tf_op jit(solution)/shard_map/while/body/eval_jaxpr/ppermute | solution.py:14
  330.6 13.8 %collective-permute-start = (bf16[128,512]{1,0:T(8,128)(2,1)S(1)}, bf16[128,512]{1,0:T(8,128)(2,1)S(1)}, u32[]{:S(2)}, u32[]{:S(2)}) collective-permute-start(bf16[128,512]{1,0:T(8,128)(2,1)S(1)} %get-tuple-element.171), channel_id=1, source_target_pairs={{0,4},{4,8},{8,12},{12,16},{16,20},{20,24},{24,28},{28,32},{32,36}... | collective-permute-start | bytes 393224 | tf_op jit(solution)/shard_map/while/body/eval_jaxpr/ppermute | solution.py:14
  332.5 11.8 %collective-permute-start.1 = (s32[128]{0:T(128)S(1)}, s32[128]{0:T(128)S(1)}, u32[]{:S(2)}, u32[]{:S(2)}) collective-permute-start(s32[128]{0:T(128)S(1)} %get-tuple-element.172), channel_id=1, source_target_pairs={{0,4},{4,8},{8,12},{12,16},{16,20},{20,24},{24,28},{28,32},{32,36}... | collective-permute-start | bytes 1544 | tf_op jit(solution)/shard_map/while/body/eval_jaxpr/ppermute | solution.py:14
  344.4 13.8 %collective-permute-start = (bf16[128,512]{1,0:T(8,128)(2,1)S(1)}, bf16[128,512]{1,0:T(8,128)(2,1)S(1)}, u32[]{:S(2)}, u32[]{:S(2)}) collective-permute-start(bf16[128,512]{1,0:T(8,128)(2,1)S(1)} %get-tuple-element.171), channel_id=1, source_target_pairs={{0,4},{4,8},{8,12},{12,16},{16,20},{20,24},{24,28},{28,32},{32,36}... | collective-permute-start | bytes 393224 | tf_op jit(solution)/shard_map/while/body/eval_jaxpr/ppermute | solution.py:14
  346.4 11.8 %collective-permute-start.1 = (s32[128]{0:T(128)S(1)}, s32[128]{0:T(128)S(1)}, u32[]{:S(2)}, u32[]{:S(2)}) collective-permute-start(s32[128]{0:T(128)S(1)} %get-tuple-element.172), channel_id=1, source_target_pairs={{0,4},{4,8},{8,12},{12,16},{16,20},{20,24},{24,28},{28,32},{32,36}... | collective-permute-start | bytes 1544 | tf_op jit(solution)/shard_map/while/body/eval_jaxpr/ppermute | solution.py:14
  358.3 13.8 %collective-permute-start = (bf16[128,512]{1,0:T(8,128)(2,1)S(1)}, bf16[128,512]{1,0:T(8,128)(2,1)S(1)}, u32[]{:S(2)}, u32[]{:S(2)}) collective-permute-start(bf16[128,512]{1,0:T(8,128)(2,1)S(1)} %get-tuple-element.171), channel_id=1, source_target_pairs={{0,4},{4,8},{8,12},{12,16},{16,20},{20,24},{24,28},{28,32},{32,36}... | collective-permute-start | bytes 393224 | tf_op jit(solution)/shard_map/while/body/eval_jaxpr/ppermute | solution.py:14
  360.2 11.8 %collective-permute-start.1 = (s32[128]{0:T(128)S(1)}, s32[128]{0:T(128)S(1)}, u32[]{:S(2)}, u32[]{:S(2)}) collective-permute-start(s32[128]{0:T(128)S(1)} %get-tuple-element.172), channel_id=1, source_target_pairs={{0,4},{4,8},{8,12},{12,16},{16,20},{20,24},{24,28},{28,32},{32,36}... | collective-permute-start | bytes 1544 | tf_op jit(solution)/shard_map/while/body/eval_jaxpr/ppermute | solution.py:14
  372.1 13.8 %collective-permute-start = (bf16[128,512]{1,0:T(8,128)(2,1)S(1)}, bf16[128,512]{1,0:T(8,128)(2,1)S(1)}, u32[]{:S(2)}, u32[]{:S(2)}) collective-permute-start(bf16[128,512]{1,0:T(8,128)(2,1)S(1)} %get-tuple-element.171), channel_id=1, source_target_pairs={{0,4},{4,8},{8,12},{12,16},{16,20},{20,24},{24,28},{28,32},{32,36}... | collective-permute-start | bytes 393224 | tf_op jit(solution)/shard_map/while/body/eval_jaxpr/ppermute | solution.py:14
  374.0 11.9 %collective-permute-start.1 = (s32[128]{0:T(128)S(1)}, s32[128]{0:T(128)S(1)}, u32[]{:S(2)}, u32[]{:S(2)}) collective-permute-start(s32[128]{0:T(128)S(1)} %get-tuple-element.172), channel_id=1, source_target_pairs={{0,4},{4,8},{8,12},{12,16},{16,20},{20,24},{24,28},{28,32},{32,36}... | collective-permute-start | bytes 1544 | tf_op jit(solution)/shard_map/while/body/eval_jaxpr/ppermute | solution.py:14
  386.0 14.9 %collective-permute-start = (bf16[128,512]{1,0:T(8,128)(2,1)S(1)}, bf16[128,512]{1,0:T(8,128)(2,1)S(1)}, u32[]{:S(2)}, u32[]{:S(2)}) collective-permute-start(bf16[128,512]{1,0:T(8,128)(2,1)S(1)} %get-tuple-element.171), channel_id=1, source_target_pairs={{0,4},{4,8},{8,12},{12,16},{16,20},{20,24},{24,28},{28,32},{32,36}... | collective-permute-start | bytes 393224 | tf_op jit(solution)/shard_map/while/body/eval_jaxpr/ppermute | solution.py:14
  387.9 12.9 %collective-permute-start.1 = (s32[128]{0:T(128)S(1)}, s32[128]{0:T(128)S(1)}, u32[]{:S(2)}, u32[]{:S(2)}) collective-permute-start(s32[128]{0:T(128)S(1)} %get-tuple-element.172), channel_id=1, source_target_pairs={{0,4},{4,8},{8,12},{12,16},{16,20},{20,24},{24,28},{28,32},{32,36}... | collective-permute-start | bytes 1544 | tf_op jit(solution)/shard_map/while/body/eval_jaxpr/ppermute | solution.py:14
  400.9 13.8 %collective-permute-start = (bf16[128,512]{1,0:T(8,128)(2,1)S(1)}, bf16[128,512]{1,0:T(8,128)(2,1)S(1)}, u32[]{:S(2)}, u32[]{:S(2)}) collective-permute-start(bf16[128,512]{1,0:T(8,128)(2,1)S(1)} %get-tuple-element.171), channel_id=1, source_target_pairs={{0,4},{4,8},{8,12},{12,16},{16,20},{20,24},{24,28},{28,32},{32,36}... | collective-permute-start | bytes 393224 | tf_op jit(solution)/shard_map/while/body/eval_jaxpr/ppermute | solution.py:14
  402.8 11.8 %collective-permute-start.1 = (s32[128]{0:T(128)S(1)}, s32[128]{0:T(128)S(1)}, u32[]{:S(2)}, u32[]{:S(2)}) collective-permute-start(s32[128]{0:T(128)S(1)} %get-tuple-element.172), channel_id=1, source_target_pairs={{0,4},{4,8},{8,12},{12,16},{16,20},{20,24},{24,28},{28,32},{32,36}... | collective-permute-start | bytes 1544 | tf_op jit(solution)/shard_map/while/body/eval_jaxpr/ppermute | solution.py:14
  414.7 13.8 %collective-permute-start = (bf16[128,512]{1,0:T(8,128)(2,1)S(1)}, bf16[128,512]{1,0:T(8,128)(2,1)S(1)}, u32[]{:S(2)}, u32[]{:S(2)}) collective-permute-start(bf16[128,512]{1,0:T(8,128)(2,1)S(1)} %get-tuple-element.171), channel_id=1, source_target_pairs={{0,4},{4,8},{8,12},{12,16},{16,20},{20,24},{24,28},{28,32},{32,36}... | collective-permute-start | bytes 393224 | tf_op jit(solution)/shard_map/while/body/eval_jaxpr/ppermute | solution.py:14
  416.7 11.8 %collective-permute-start.1 = (s32[128]{0:T(128)S(1)}, s32[128]{0:T(128)S(1)}, u32[]{:S(2)}, u32[]{:S(2)}) collective-permute-start(s32[128]{0:T(128)S(1)} %get-tuple-element.172), channel_id=1, source_target_pairs={{0,4},{4,8},{8,12},{12,16},{16,20},{20,24},{24,28},{28,32},{32,36}... | collective-permute-start | bytes 1544 | tf_op jit(solution)/shard_map/while/body/eval_jaxpr/ppermute | solution.py:14
  428.6 13.8 %collective-permute-start = (bf16[128,512]{1,0:T(8,128)(2,1)S(1)}, bf16[128,512]{1,0:T(8,128)(2,1)S(1)}, u32[]{:S(2)}, u32[]{:S(2)}) collective-permute-start(bf16[128,512]{1,0:T(8,128)(2,1)S(1)} %get-tuple-element.171), channel_id=1, source_target_pairs={{0,4},{4,8},{8,12},{12,16},{16,20},{20,24},{24,28},{28,32},{32,36}... | collective-permute-start | bytes 393224 | tf_op jit(solution)/shard_map/while/body/eval_jaxpr/ppermute | solution.py:14
  430.5 11.8 %collective-permute-start.1 = (s32[128]{0:T(128)S(1)}, s32[128]{0:T(128)S(1)}, u32[]{:S(2)}, u32[]{:S(2)}) collective-permute-start(s32[128]{0:T(128)S(1)} %get-tuple-element.172), channel_id=1, source_target_pairs={{0,4},{4,8},{8,12},{12,16},{16,20},{20,24},{24,28},{28,32},{32,36}... | collective-permute-start | bytes 1544 | tf_op jit(solution)/shard_map/while/body/eval_jaxpr/ppermute | solution.py:14
  442.4 13.8 %collective-permute-start = (bf16[128,512]{1,0:T(8,128)(2,1)S(1)}, bf16[128,512]{1,0:T(8,128)(2,1)S(1)}, u32[]{:S(2)}, u32[]{:S(2)}) collective-permute-start(bf16[128,512]{1,0:T(8,128)(2,1)S(1)} %get-tuple-element.171), channel_id=1, source_target_pairs={{0,4},{4,8},{8,12},{12,16},{16,20},{20,24},{24,28},{28,32},{32,36}... | collective-permute-start | bytes 393224 | tf_op jit(solution)/shard_map/while/body/eval_jaxpr/ppermute | solution.py:14
  444.3 11.8 %collective-permute-start.1 = (s32[128]{0:T(128)S(1)}, s32[128]{0:T(128)S(1)}, u32[]{:S(2)}, u32[]{:S(2)}) collective-permute-start(s32[128]{0:T(128)S(1)} %get-tuple-element.172), channel_id=1, source_target_pairs={{0,4},{4,8},{8,12},{12,16},{16,20},{20,24},{24,28},{28,32},{32,36}... | collective-permute-start | bytes 1544 | tf_op jit(solution)/shard_map/while/body/eval_jaxpr/ppermute | solution.py:14
  456.2 13.8 %collective-permute-start = (bf16[128,512]{1,0:T(8,128)(2,1)S(1)}, bf16[128,512]{1,0:T(8,128)(2,1)S(1)}, u32[]{:S(2)}, u32[]{:S(2)}) collective-permute-start(bf16[128,512]{1,0:T(8,128)(2,1)S(1)} %get-tuple-element.171), channel_id=1, source_target_pairs={{0,4},{4,8},{8,12},{12,16},{16,20},{20,24},{24,28},{28,32},{32,36}... | collective-permute-start | bytes 393224 | tf_op jit(solution)/shard_map/while/body/eval_jaxpr/ppermute | solution.py:14
  458.1 11.8 %collective-permute-start.1 = (s32[128]{0:T(128)S(1)}, s32[128]{0:T(128)S(1)}, u32[]{:S(2)}, u32[]{:S(2)}) collective-permute-start(s32[128]{0:T(128)S(1)} %get-tuple-element.172), channel_id=1, source_target_pairs={{0,4},{4,8},{8,12},{12,16},{16,20},{20,24},{24,28},{28,32},{32,36}... | collective-permute-start | bytes 1544 | tf_op jit(solution)/shard_map/while/body/eval_jaxpr/ppermute | solution.py:14
  470.0 13.8 %collective-permute-start = (bf16[128,512]{1,0:T(8,128)(2,1)S(1)}, bf16[128,512]{1,0:T(8,128)(2,1)S(1)}, u32[]{:S(2)}, u32[]{:S(2)}) collective-permute-start(bf16[128,512]{1,0:T(8,128)(2,1)S(1)} %get-tuple-element.171), channel_id=1, source_target_pairs={{0,4},{4,8},{8,12},{12,16},{16,20},{20,24},{24,28},{28,32},{32,36}... | collective-permute-start | bytes 393224 | tf_op jit(solution)/shard_map/while/body/eval_jaxpr/ppermute | solution.py:14
  472.0 11.8 %collective-permute-start.1 = (s32[128]{0:T(128)S(1)}, s32[128]{0:T(128)S(1)}, u32[]{:S(2)}, u32[]{:S(2)}) collective-permute-start(s32[128]{0:T(128)S(1)} %get-tuple-element.172), channel_id=1, source_target_pairs={{0,4},{4,8},{8,12},{12,16},{16,20},{20,24},{24,28},{28,32},{32,36}... | collective-permute-start | bytes 1544 | tf_op jit(solution)/shard_map/while/body/eval_jaxpr/ppermute | solution.py:14
  483.9 13.8 %collective-permute-start = (bf16[128,512]{1,0:T(8,128)(2,1)S(1)}, bf16[128,512]{1,0:T(8,128)(2,1)S(1)}, u32[]{:S(2)}, u32[]{:S(2)}) collective-permute-start(bf16[128,512]{1,0:T(8,128)(2,1)S(1)} %get-tuple-element.171), channel_id=1, source_target_pairs={{0,4},{4,8},{8,12},{12,16},{16,20},{20,24},{24,28},{28,32},{32,36}... | collective-permute-start | bytes 393224 | tf_op jit(solution)/shard_map/while/body/eval_jaxpr/ppermute | solution.py:14
  485.8 11.8 %collective-permute-start.1 = (s32[128]{0:T(128)S(1)}, s32[128]{0:T(128)S(1)}, u32[]{:S(2)}, u32[]{:S(2)}) collective-permute-start(s32[128]{0:T(128)S(1)} %get-tuple-element.172), channel_id=1, source_target_pairs={{0,4},{4,8},{8,12},{12,16},{16,20},{20,24},{24,28},{28,32},{32,36}... | collective-permute-start | bytes 1544 | tf_op jit(solution)/shard_map/while/body/eval_jaxpr/ppermute | solution.py:14
  497.7 13.8 %collective-permute-start = (bf16[128,512]{1,0:T(8,128)(2,1)S(1)}, bf16[128,512]{1,0:T(8,128)(2,1)S(1)}, u32[]{:S(2)}, u32[]{:S(2)}) collective-permute-start(bf16[128,512]{1,0:T(8,128)(2,1)S(1)} %get-tuple-element.171), channel_id=1, source_target_pairs={{0,4},{4,8},{8,12},{12,16},{16,20},{20,24},{24,28},{28,32},{32,36}... | collective-permute-start | bytes 393224 | tf_op jit(solution)/shard_map/while/body/eval_jaxpr/ppermute | solution.py:14
  499.6 11.8 %collective-permute-start.1 = (s32[128]{0:T(128)S(1)}, s32[128]{0:T(128)S(1)}, u32[]{:S(2)}, u32[]{:S(2)}) collective-permute-start(s32[128]{0:T(128)S(1)} %get-tuple-element.172), channel_id=1, source_target_pairs={{0,4},{4,8},{8,12},{12,16},{16,20},{20,24},{24,28},{28,32},{32,36}... | collective-permute-start | bytes 1544 | tf_op jit(solution)/shard_map/while/body/eval_jaxpr/ppermute | solution.py:14
  511.5 0.6 copy-start.9
  519.7 35.5 %copy-start = (bf16[128,640]{1,0:T(8,128)(2,1)S(1)}, bf16[128,640]{1,0:T(8,128)(2,1)}, u32[]{:S(2)}) copy-start(bf16[128,640]{1,0:T(8,128)(2,1)} %param.8) | copy-start | bytes 491524
Sparse Core Ops, SparseCore 0:
  12.7 135.2 all-gather.6
  152.7 127.3 all-gather.8
  284.8 126.9 all-gather.10
  521.0 33.1 reduce-scatter.3
where the time goes:
time: 564 us; the launch traced here: 562 us
  waiting for transfers between devices  406 us (72%)
  starting transfers between devices  62.4 us (11%)
  blocking collectives  50.3 us (9%)
  local copies, waits for them, and re-layouts  16.6 us (3%)
  between operations  14.1 us (2%)
  other arithmetic  6.51 us (1%)
  matrix products  5.67 us (1%)
    ppermute x32, waiting for transfers between devices, from_behind(): return lax.ppermute(x, axis, pairs)  160 us
    all_gather x1, waiting for transfers between devices, per_device(): lax.all_gather(w_query, 'seq', axis=0, tiled=True)  125 us
    all_gather x1, waiting for transfers between devices, per_device(): lax.all_gather(w_keyval, 'seq', axis=0, tiled=True)  85.6 us
    ppermute x32, starting transfers between devices, from_behind(): return lax.ppermute(x, axis, pairs)  62.3 us
    unnamed x5, waiting for transfers between devices  35.4 us
    psum x1, blocking collectives, per_device(): starts = lax.psum(below, 'seq')  31.9 us
    all_gather x1, blocking collectives, per_device(): gathered = lax.all_gather(tokens, 'tp', axis=1, tiled=True)  18.5 us
    unnamed x27, local copies, waits for them, and re-layouts  13.8 us
  transfers between devices with their start and end apart: 36, of which 19 were waited for; matrix products, arithmetic and copies ran while one was open for 4% of the time, Pallas kernels for 0%

commit v1 on v0

--- a/solution.py
+++ b/solution.py
@@ -53,7 +53,9 @@
     positions = (token_index - own_start).astype(jnp.float32)
     query_raw = jnp.dot(
         normed,
-        lax.all_gather(w_query, "seq", axis=0, tiled=True),
+        jnp.concatenate(
+            lax.all_to_all(jnp.stack([w_query] * lax.axis_size("seq")), "seq", 0, 0), axis=0
+        ),
         preferred_element_type=jnp.float32,
     )
     keyval_raw = jnp.dot(

time: 564 us -> 612 us (1.085)
  waiting for transfers between devices: 406 us -> 345 us
  blocking collectives: 50.3 us -> 109 us
  local copies, waits for them, and re-layouts: 16.6 us -> 47.7 us
  starting transfers between devices: 62.4 us -> 82.2 us
    all_gather x1 -> x0, waiting for transfers between devices: 125 us -> none  [per_device(): lax.all_gather(w_query, 'seq', axis=0, tiled=True)]
    all_gather x1, waiting for transfers between devices: 0.02 us -> 121 us  [per_device(): lax.all_gather(w_out, 'seq', axis=1, tiled=True)]
    psum x1, blocking collectives: 31.9 us -> 93 us  [per_device(): starts = lax.psum(below, 'seq')]
    all_gather x1, waiting for transfers between devices: 85.6 us -> 38.9 us  [per_device(): lax.all_gather(w_keyval, 'seq', axis=0, tiled=True)]
    all_to_all x0 -> x1, starting transfers between devices: none -> 20.1 us  [per_device(): lax.all_to_all(jnp.stack([w_query] * lax.axis_size('seq')), 'seq', 0, 0)]
    while x32, local copies, waits for them, and re-layouts: 0.19 us -> 10.6 us
    dynamic_update_slice x16, local copies, waits for them, and re-layouts: 0.25 us -> 10.6 us  [advance(): store = lax.dynamic_update_slice_in_dim(store, current[None], slot, 0)]
    unnamed x5 -> x4, waiting for transfers between devices: 35.4 us -> 26.3 us
  transfers between devices with their start and end apart: 36 -> 36, of which waited for: 19 -> 19; matrix products, arithmetic and copies ran while one was open for 4% -> 7% of each run, Pallas kernels for 0% -> 0%
where the time goes in v1:
time: 612 us; the launch traced here: 610 us
  waiting for transfers between devices  345 us (56%)
  blocking collectives  109 us (18%)
  starting transfers between devices  82.2 us (13%)
  local copies, waits for them, and re-layouts  47.7 us (8%)
  between operations  14 us (2%)
  matrix products  7.4 us (1%)
    ppermute x32, waiting for transfers between devices, from_behind(): return lax.ppermute(x, axis, pairs)  159 us
    all_gather x1, waiting for transfers between devices, per_device(): lax.all_gather(w_out, 'seq', axis=1, tiled=True)  121 us
    psum x1, blocking collectives, per_device(): starts = lax.psum(below, 'seq')  93 us
    ppermute x32, starting transfers between devices, from_behind(): return lax.ppermute(x, axis, pairs)  61.9 us
    all_gather x1, waiting for transfers between devices, per_device(): lax.all_gather(w_keyval, 'seq', axis=0, tiled=True)  38.9 us
    unnamed x4, waiting for transfers between devices  26.3 us
    all_to_all x1, starting transfers between devices, per_device(): lax.all_to_all(jnp.stack([w_query] * lax.axis_size('seq')), 'seq', 0, 0)  20.1 us
    unnamed x35, local copies, waits for them, and re-layouts  15.8 us
  transfers between devices with their start and end apart: 36, of which 19 were waited for; matrix products, arithmetic and copies ran while one was open for 7% of the time, Pallas kernels for 0%

profile of v1, /device:TPU:2, one launch (start us, length us, event | category | flops | bytes accessed | tf_op | source)
XLA Modules:
  0.0 610.5 jit_solution(13516661169871425369)
XLA Ops:
  8.6 2.6 stack.2
  11.2 20.1 %all-to-all-start = ((bf16[128,20,512]{2,1,0:T(8,128)(2,1)}), bf16[128,20,512]{2,1,0:T(8,128)(2,1)S(1)}, u32[]{:S(2)}, u32[]{:S(2)}) async-start(bf16[128,20,512]{2,1,0:T(8,128)(2,1)} %stack.2), calls=%async_computation | async-start | bytes 6291456 | tf_op jit(solution)/shard_map/all_to_all | solution.py:57
  31.6 93.0 %psum.7 = s32[32]{0:T(128)S(1)} all-reduce(s32[32]{0:T(128)S(1)} %convert_reduce_fusion), channel_id=1, replica_groups=mesh['seq'=128,'tp'=4] {'seq'}, use_global_device_ids=true, to_apply=%region_2.0 | all-reduce | flops 32 | bytes 256 | tf_op jit(solution)/shard_map/psum | solution.py:50
  124.6 15.7 %all_gather.9 = bf16[128,2560]{1,0:T(8,128)(2,1)S(1)} all-gather(bf16[128,640]{1,0:T(8,128)(2,1)S(1)} %copy-done.4), channel_id=1, replica_groups=mesh['seq'=128,'tp'=4] {'tp'}, dimensions={1}, use_global_device_ids=true | all-gather | bytes 819200 | tf_op jit(solution)/shard_map/all_gather | solution.py:45
  142.8 38.9 %all-gather.5.cloned.1.call-done = bf16[128,20,512]{2,1,0:T(8,128)(2,1)} async-done(((bf16[1,20,512]{2,1,0:T(8,128)(2,1)}), bf16[128,20,512]{2,1,0:T(8,128)(2,1)}) %all-gather.5.cloned.1.call-update) | async-done | bytes 2621456 | tf_op jit(solution)/shard_map/all_gather | solution.py:63
  181.7 5.2 reshape.168
  186.9 3.1 fusion.17
  192.7 121.1 %all-gather.7.cloned.1.call-done = bf16[128,20,512]{2,1,0:T(8,128)(2,1)} async-done(((bf16[1,20,512]{2,1,0:T(8,128)(2,1)}), bf16[128,20,512]{2,1,0:T(8,128)(2,1)}) %all-gather.7.cloned.1.call-update) | async-done | bytes 2621456 | tf_op jit(solution)/shard_map/all_gather | solution.py:110
  313.8 5.2 reshape.170
  319.0 1.5 broadcast_in_dim.65
  320.6 242.8 %while.19 = (s32[]{:T(128)}, bf16[128,512]{1,0:T(8,128)(2,1)}, s32[128]{0:T(128)S(1)}, bf16[16,128,512]{2,1,0:T(8,128)(2,1)}, s32[16,128]{1,0:T(8,128)S(1)}, /*index=5*/s32[]{:T(128)}, s32[]{:T(128)}, s32[]{:T(128)}, s32[]{:T(128)}) while((s32[]{:T(128)}, bf16[128,512]{1,0:T(8,128)(2,1)}, s32[128]{0:T(128)S(1)}, ...), condition=%wide.region_5.6_spmd, body=%wide.region_4.5_spmd.sunk | while | flops 6 | bytes 1052899 | solution.py:82
  320.6 2.1 collective-permute-start
  322.7 2.4 collective-permute-start.1
  325.1 9.4 %collective-permute-done.1 = s32[128]{0:T(128)S(1)} collective-permute-done((s32[128]{0:T(128)S(1)}, s32[128]{0:T(128)S(1)}, u32[]{:S(2)}, u32[]{:S(2)}) %collective-permute-start.1) | collective-permute-done | bytes 544 | tf_op jit(solution)/shard_map/while/body/eval_jaxpr/ppermute | solution.py:14
  335.8 1.9 collective-permute-start
  337.8 1.9 collective-permute-start.1
  339.7 9.9 %collective-permute-done.1 = s32[128]{0:T(128)S(1)} collective-permute-done((s32[128]{0:T(128)S(1)}, s32[128]{0:T(128)S(1)}, u32[]{:S(2)}, u32[]{:S(2)}) %collective-permute-start.1) | collective-permute-done | bytes 544 | tf_op jit(solution)/shard_map/while/body/eval_jaxpr/ppermute | solution.py:14
  350.9 1.9 collective-permute-start
  352.8 1.9 collective-permute-start.1
  354.8 11.1 %collective-permute-done.1 = s32[128]{0:T(128)S(1)} collective-permute-done((s32[128]{0:T(128)S(1)}, s32[128]{0:T(128)S(1)}, u32[]{:S(2)}, u32[]{:S(2)}) %collective-permute-start.1) | collective-permute-done | bytes 544 | tf_op jit(solution)/shard_map/while/body/eval_jaxpr/ppermute | solution.py:14
  367.3 1.9 collective-permute-start
  369.2 1.9 collective-permute-start.1
  371.1 9.9 %collective-permute-done.1 = s32[128]{0:T(128)S(1)} collective-permute-done((s32[128]{0:T(128)S(1)}, s32[128]{0:T(128)S(1)}, u32[]{:S(2)}, u32[]{:S(2)}) %collective-permute-start.1) | collective-permute-done | bytes 544 | tf_op jit(solution)/shard_map/while/body/eval_jaxpr/ppermute | solution.py:14
  382.4 1.9 collective-permute-start
  384.3 1.9 collective-permute-start.1
  386.2 9.9 %collective-permute-done.1 = s32[128]{0:T(128)S(1)} collective-permute-done((s32[128]{0:T(128)S(1)}, s32[128]{0:T(128)S(1)}, u32[]{:S(2)}, u32[]{:S(2)}) %collective-permute-start.1) | collective-permute-done | bytes 544 | tf_op jit(solution)/shard_map/while/body/eval_jaxpr/ppermute | solution.py:14
  397.4 1.9 collective-permute-start
  399.4 1.9 collective-permute-start.1
  401.3 9.9 %collective-permute-done.1 = s32[128]{0:T(128)S(1)} collective-permute-done((s32[128]{0:T(128)S(1)}, s32[128]{0:T(128)S(1)}, u32[]{:S(2)}, u32[]{:S(2)}) %collective-permute-start.1) | collective-permute-done | bytes 544 | tf_op jit(solution)/shard_map/while/body/eval_jaxpr/ppermute | solution.py:14
  412.5 1.9 collective-permute-start
  414.4 1.9 collective-permute-start.1
  416.4 9.9 %collective-permute-done.1 = s32[128]{0:T(128)S(1)} collective-permute-done((s32[128]{0:T(128)S(1)}, s32[128]{0:T(128)S(1)}, u32[]{:S(2)}, u32[]{:S(2)}) %collective-permute-start.1) | collective-permute-done | bytes 544 | tf_op jit(solution)/shard_map/while/body/eval_jaxpr/ppermute | solution.py:14
  427.6 1.9 collective-permute-start
  429.5 1.9 collective-permute-start.1
  431.5 9.9 %collective-permute-done.1 = s32[128]{0:T(128)S(1)} collective-permute-done((s32[128]{0:T(128)S(1)}, s32[128]{0:T(128)S(1)}, u32[]{:S(2)}, u32[]{:S(2)}) %collective-permute-start.1) | collective-permute-done | bytes 544 | tf_op jit(solution)/shard_map/while/body/eval_jaxpr/ppermute | solution.py:14
  442.7 1.9 collective-permute-start
  444.6 1.9 collective-permute-start.1
  446.5 9.9 %collective-permute-done.1 = s32[128]{0:T(128)S(1)} collective-permute-done((s32[128]{0:T(128)S(1)}, s32[128]{0:T(128)S(1)}, u32[]{:S(2)}, u32[]{:S(2)}) %collective-permute-start.1) | collective-permute-done | bytes 544 | tf_op jit(solution)/shard_map/while/body/eval_jaxpr/ppermute | solution.py:14
  457.8 1.9 collective-permute-start
  459.7 1.9 collective-permute-start.1
  461.6 9.9 %collective-permute-done.1 = s32[128]{0:T(128)S(1)} collective-permute-done((s32[128]{0:T(128)S(1)}, s32[128]{0:T(128)S(1)}, u32[]{:S(2)}, u32[]{:S(2)}) %collective-permute-start.1) | collective-permute-done | bytes 544 | tf_op jit(solution)/shard_map/while/body/eval_jaxpr/ppermute | solution.py:14
  472.8 1.9 collective-permute-start
  474.8 1.9 collective-permute-start.1
  476.7 9.9 %collective-permute-done.1 = s32[128]{0:T(128)S(1)} collective-permute-done((s32[128]{0:T(128)S(1)}, s32[128]{0:T(128)S(1)}, u32[]{:S(2)}, u32[]{:S(2)}) %collective-permute-start.1) | collective-permute-done | bytes 544 | tf_op jit(solution)/shard_map/while/body/eval_jaxpr/ppermute | solution.py:14
  487.9 1.9 collective-permute-start
  489.8 1.9 collective-permute-start.1
  491.8 9.9 %collective-permute-done.1 = s32[128]{0:T(128)S(1)} collective-permute-done((s32[128]{0:T(128)S(1)}, s32[128]{0:T(128)S(1)}, u32[]{:S(2)}, u32[]{:S(2)}) %collective-permute-start.1) | collective-permute-done | bytes 544 | tf_op jit(solution)/shard_map/while/body/eval_jaxpr/ppermute | solution.py:14
  503.0 1.9 collective-permute-start
  504.9 1.9 collective-permute-start.1
  506.8 9.9 %collective-permute-done.1 = s32[128]{0:T(128)S(1)} collective-permute-done((s32[128]{0:T(128)S(1)}, s32[128]{0:T(128)S(1)}, u32[]{:S(2)}, u32[]{:S(2)}) %collective-permute-start.1) | collective-permute-done | bytes 544 | tf_op jit(solution)/shard_map/while/body/eval_jaxpr/ppermute | solution.py:14
  518.1 1.9 collective-permute-start
  520.0 1.9 collective-permute-start.1
  521.9 9.9 %collective-permute-done.1 = s32[128]{0:T(128)S(1)} collective-permute-done((s32[128]{0:T(128)S(1)}, s32[128]{0:T(128)S(1)}, u32[]{:S(2)}, u32[]{:S(2)}) %collective-permute-start.1) | collective-permute-done | bytes 544 | tf_op jit(solution)/shard_map/while/body/eval_jaxpr/ppermute | solution.py:14
  533.2 1.9 collective-permute-start
  535.1 1.9 collective-permute-start.1
  537.0 9.9 %collective-permute-done.1 = s32[128]{0:T(128)S(1)} collective-permute-done((s32[128]{0:T(128)S(1)}, s32[128]{0:T(128)S(1)}, u32[]{:S(2)}, u32[]{:S(2)}) %collective-permute-start.1) | collective-permute-done | bytes 544 | tf_op jit(solution)/shard_map/while/body/eval_jaxpr/ppermute | solution.py:14
  548.3 1.9 collective-permute-start
  550.2 1.9 collective-permute-start.1
  552.1 9.9 %collective-permute-done.1 = s32[128]{0:T(128)S(1)} collective-permute-done((s32[128]{0:T(128)S(1)}, s32[128]{0:T(128)S(1)}, u32[]{:S(2)}, u32[]{:S(2)}) %collective-permute-start.1) | collective-permute-done | bytes 544 | tf_op jit(solution)/shard_map/while/body/eval_jaxpr/ppermute | solution.py:14
  564.0 2.2 reshape.165
  566.2 3.0 copy.15
  573.9 1.3 copy-done
  576.2 1.1 copy.19
  577.3 24.9 %reduce-scatter.4.cloned.1.call-done = bf16[640,128]{1,0:T(8,128)(2,1)} async-done(((bf16[2560,128]{1,0:T(8,128)(2,1)}), bf16[640,128]{1,0:T(8,128)(2,1)}) %reduce-scatter.4.cloned.1.call-update) | async-done | bytes 163856
  (149 shorter events, 36.4 us)
Async XLA Ops:
  7.2 174.6 %all-gather.5.cloned.1.call-start = ((), (), s32[]{:S(2)}) async-start(), calls=%async_computation.2 | async-start | bytes 3170304 | tf_op jit(solution)/shard_map/all_gather | solution.py:63
  7.9 305.9 %all-gather.7.cloned.1.call-start = ((), (), s32[]{:S(2)}) async-start(), calls=%async_computation.3 | async-start | bytes 3170304 | tf_op jit(solution)/shard_map/all_gather | solution.py:110
  11.2 20.2 %copy-start.11 = (s32[128]{0:T(128)S(1)}, s32[128]{0:T(128)}, u32[]{:S(2)}) copy-start(s32[128]{0:T(128)} %param.9) | copy-start | bytes 1540
  11.2 113.4 %copy-start.4 = (bf16[128,640]{1,0:T(8,128)(2,1)S(1)}, bf16[128,640]{1,0:T(8,128)(2,1)}, u32[]{:S(2)}) copy-start(bf16[128,640]{1,0:T(8,128)(2,1)} %param.8) | copy-start | bytes 491524
  11.2 552.8 %all-to-all-start = ((bf16[128,20,512]{2,1,0:T(8,128)(2,1)}), bf16[128,20,512]{2,1,0:T(8,128)(2,1)S(1)}, u32[]{:S(2)}, u32[]{:S(2)}) async-start(bf16[128,20,512]{2,1,0:T(8,128)(2,1)} %stack.2), calls=%async_computation | async-start | bytes 6291456 | tf_op jit(solution)/shard_map/all_to_all | solution.py:57
  31.4 110.5 %copy-start.8 = (bf16[2560]{0:T(1024)(128)(2,1)S(1)}, bf16[2560]{0:T(1024)(128)(2,1)}, u32[]{:S(2)}) copy-start(bf16[2560]{0:T(1024)(128)(2,1)} %param.10) | copy-start | bytes 15364
  31.4 570.8 %reduce-scatter.4.cloned.1.call-start = ((), (), s32[]{:S(2)}) async-start(), calls=%async_computation.4 | async-start | bytes 819200
  140.3 0.8 copy-start.1
  141.3 45.6 %copy-start.9 = (f32[128]{0:T(128)}, f32[128]{0:T(128)S(1)}, u32[]{:S(2)}) copy-start(f32[128]{0:T(128)S(1)} %add_rsqrt_fusion) | copy-start | bytes 1540
  192.0 127.0 %copy-start.5 = (bf16[128,512]{1,0:T(8,128)(2,1)}, bf16[128,512]{1,0:T(8,128)(2,1)S(1)}, u32[]{:S(2)}) copy-start(bf16[128,512]{1,0:T(8,128)(2,1)S(1)} %copy.14) | copy-start | bytes 393220
  319.0 1.6 copy-start.13
  320.6 14.0 %collective-permute-start = (bf16[128,512]{1,0:T(8,128)(2,1)}, bf16[128,512]{1,0:T(8,128)(2,1)S(1)}, u32[]{:S(2)}, u32[]{:S(2)}) collective-permute-start(bf16[128,512]{1,0:T(8,128)(2,1)} %get-tuple-element.169), channel_id=1, source_target_pairs={{0,4},{4,8},{8,12},{12,16},{16,20},{20,24},{24,28},{28,32},{32,36}... | collective-permute-start | bytes 393224 | tf_op jit(solution)/shard_map/while/body/eval_jaxpr/ppermute | solution.py:14
  322.7 11.8 %collective-permute-start.1 = (s32[128]{0:T(128)S(1)}, s32[128]{0:T(128)S(1)}, u32[]{:S(2)}, u32[]{:S(2)}) collective-permute-start(s32[128]{0:T(128)S(1)} %get-tuple-element.170), channel_id=1, source_target_pairs={{0,4},{4,8},{8,12},{12,16},{16,20},{20,24},{24,28},{28,32},{32,36}... | collective-permute-start | bytes 1544 | tf_op jit(solution)/shard_map/while/body/eval_jaxpr/ppermute | solution.py:14
  335.8 13.8 %collective-permute-start = (bf16[128,512]{1,0:T(8,128)(2,1)}, bf16[128,512]{1,0:T(8,128)(2,1)S(1)}, u32[]{:S(2)}, u32[]{:S(2)}) collective-permute-start(bf16[128,512]{1,0:T(8,128)(2,1)} %get-tuple-element.169), channel_id=1, source_target_pairs={{0,4},{4,8},{8,12},{12,16},{16,20},{20,24},{24,28},{28,32},{32,36}... | collective-permute-start | bytes 393224 | tf_op jit(solution)/shard_map/while/body/eval_jaxpr/ppermute | solution.py:14
  337.8 11.8 %collective-permute-start.1 = (s32[128]{0:T(128)S(1)}, s32[128]{0:T(128)S(1)}, u32[]{:S(2)}, u32[]{:S(2)}) collective-permute-start(s32[128]{0:T(128)S(1)} %get-tuple-element.170), channel_id=1, source_target_pairs={{0,4},{4,8},{8,12},{12,16},{16,20},{20,24},{24,28},{28,32},{32,36}... | collective-permute-start | bytes 1544 | tf_op jit(solution)/shard_map/while/body/eval_jaxpr/ppermute | solution.py:14
  350.9 15.0 %collective-permute-start = (bf16[128,512]{1,0:T(8,128)(2,1)}, bf16[128,512]{1,0:T(8,128)(2,1)S(1)}, u32[]{:S(2)}, u32[]{:S(2)}) collective-permute-start(bf16[128,512]{1,0:T(8,128)(2,1)} %get-tuple-element.169), channel_id=1, source_target_pairs={{0,4},{4,8},{8,12},{12,16},{16,20},{20,24},{24,28},{28,32},{32,36}... | collective-permute-start | bytes 393224 | tf_op jit(solution)/shard_map/while/body/eval_jaxpr/ppermute | solution.py:14
  352.8 13.1 %collective-permute-start.1 = (s32[128]{0:T(128)S(1)}, s32[128]{0:T(128)S(1)}, u32[]{:S(2)}, u32[]{:S(2)}) collective-permute-start(s32[128]{0:T(128)S(1)} %get-tuple-element.170), channel_id=1, source_target_pairs={{0,4},{4,8},{8,12},{12,16},{16,20},{20,24},{24,28},{28,32},{32,36}... | collective-permute-start | bytes 1544 | tf_op jit(solution)/shard_map/while/body/eval_jaxpr/ppermute | solution.py:14
  367.3 13.8 %collective-permute-start = (bf16[128,512]{1,0:T(8,128)(2,1)}, bf16[128,512]{1,0:T(8,128)(2,1)S(1)}, u32[]{:S(2)}, u32[]{:S(2)}) collective-permute-start(bf16[128,512]{1,0:T(8,128)(2,1)} %get-tuple-element.169), channel_id=1, source_target_pairs={{0,4},{4,8},{8,12},{12,16},{16,20},{20,24},{24,28},{28,32},{32,36}... | collective-permute-start | bytes 393224 | tf_op jit(solution)/shard_map/while/body/eval_jaxpr/ppermute | solution.py:14
  369.2 11.8 %collective-permute-start.1 = (s32[128]{0:T(128)S(1)}, s32[128]{0:T(128)S(1)}, u32[]{:S(2)}, u32[]{:S(2)}) collective-permute-start(s32[128]{0:T(128)S(1)} %get-tuple-element.170), channel_id=1, source_target_pairs={{0,4},{4,8},{8,12},{12,16},{16,20},{20,24},{24,28},{28,32},{32,36}... | collective-permute-start | bytes 1544 | tf_op jit(solution)/shard_map/while/body/eval_jaxpr/ppermute | solution.py:14
  382.4 13.8 %collective-permute-start = (bf16[128,512]{1,0:T(8,128)(2,1)}, bf16[128,512]{1,0:T(8,128)(2,1)S(1)}, u32[]{:S(2)}, u32[]{:S(2)}) collective-permute-start(bf16[128,512]{1,0:T(8,128)(2,1)} %get-tuple-element.169), channel_id=1, source_target_pairs={{0,4},{4,8},{8,12},{12,16},{16,20},{20,24},{24,28},{28,32},{32,36}... | collective-permute-start | bytes 393224 | tf_op jit(solution)/shard_map/while/body/eval_jaxpr/ppermute | solution.py:14
  384.3 11.8 %collective-permute-start.1 = (s32[128]{0:T(128)S(1)}, s32[128]{0:T(128)S(1)}, u32[]{:S(2)}, u32[]{:S(2)}) collective-permute-start(s32[128]{0:T(128)S(1)} %get-tuple-element.170), channel_id=1, source_target_pairs={{0,4},{4,8},{8,12},{12,16},{16,20},{20,24},{24,28},{28,32},{32,36}... | collective-permute-start | bytes 1544 | tf_op jit(solution)/shard_map/while/body/eval_jaxpr/ppermute | solution.py:14
  397.4 13.8 %collective-permute-start = (bf16[128,512]{1,0:T(8,128)(2,1)}, bf16[128,512]{1,0:T(8,128)(2,1)S(1)}, u32[]{:S(2)}, u32[]{:S(2)}) collective-permute-start(bf16[128,512]{1,0:T(8,128)(2,1)} %get-tuple-element.169), channel_id=1, source_target_pairs={{0,4},{4,8},{8,12},{12,16},{16,20},{20,24},{24,28},{28,32},{32,36}... | collective-permute-start | bytes 393224 | tf_op jit(solution)/shard_map/while/body/eval_jaxpr/ppermute | solution.py:14
  399.4 11.8 %collective-permute-start.1 = (s32[128]{0:T(128)S(1)}, s32[128]{0:T(128)S(1)}, u32[]{:S(2)}, u32[]{:S(2)}) collective-permute-start(s32[128]{0:T(128)S(1)} %get-tuple-element.170), channel_id=1, source_target_pairs={{0,4},{4,8},{8,12},{12,16},{16,20},{20,24},{24,28},{28,32},{32,36}... | collective-permute-start | bytes 1544 | tf_op jit(solution)/shard_map/while/body/eval_jaxpr/ppermute | solution.py:14
  412.5 13.8 %collective-permute-start = (bf16[128,512]{1,0:T(8,128)(2,1)}, bf16[128,512]{1,0:T(8,128)(2,1)S(1)}, u32[]{:S(2)}, u32[]{:S(2)}) collective-permute-start(bf16[128,512]{1,0:T(8,128)(2,1)} %get-tuple-element.169), channel_id=1, source_target_pairs={{0,4},{4,8},{8,12},{12,16},{16,20},{20,24},{24,28},{28,32},{32,36}... | collective-permute-start | bytes 393224 | tf_op jit(solution)/shard_map/while/body/eval_jaxpr/ppermute | solution.py:14
  414.4 11.8 %collective-permute-start.1 = (s32[128]{0:T(128)S(1)}, s32[128]{0:T(128)S(1)}, u32[]{:S(2)}, u32[]{:S(2)}) collective-permute-start(s32[128]{0:T(128)S(1)} %get-tuple-element.170), channel_id=1, source_target_pairs={{0,4},{4,8},{8,12},{12,16},{16,20},{20,24},{24,28},{28,32},{32,36}... | collective-permute-start | bytes 1544 | tf_op jit(solution)/shard_map/while/body/eval_jaxpr/ppermute | solution.py:14
  427.6 13.8 %collective-permute-start = (bf16[128,512]{1,0:T(8,128)(2,1)}, bf16[128,512]{1,0:T(8,128)(2,1)S(1)}, u32[]{:S(2)}, u32[]{:S(2)}) collective-permute-start(bf16[128,512]{1,0:T(8,128)(2,1)} %get-tuple-element.169), channel_id=1, source_target_pairs={{0,4},{4,8},{8,12},{12,16},{16,20},{20,24},{24,28},{28,32},{32,36}... | collective-permute-start | bytes 393224 | tf_op jit(solution)/shard_map/while/body/eval_jaxpr/ppermute | solution.py:14
  429.5 11.8 %collective-permute-start.1 = (s32[128]{0:T(128)S(1)}, s32[128]{0:T(128)S(1)}, u32[]{:S(2)}, u32[]{:S(2)}) collective-permute-start(s32[128]{0:T(128)S(1)} %get-tuple-element.170), channel_id=1, source_target_pairs={{0,4},{4,8},{8,12},{12,16},{16,20},{20,24},{24,28},{28,32},{32,36}... | collective-permute-start | bytes 1544 | tf_op jit(solution)/shard_map/while/body/eval_jaxpr/ppermute | solution.py:14
  442.7 13.8 %collective-permute-start = (bf16[128,512]{1,0:T(8,128)(2,1)}, bf16[128,512]{1,0:T(8,128)(2,1)S(1)}, u32[]{:S(2)}, u32[]{:S(2)}) collective-permute-start(bf16[128,512]{1,0:T(8,128)(2,1)} %get-tuple-element.169), channel_id=1, source_target_pairs={{0,4},{4,8},{8,12},{12,16},{16,20},{20,24},{24,28},{28,32},{32,36}... | collective-permute-start | bytes 393224 | tf_op jit(solution)/shard_map/while/body/eval_jaxpr/ppermute | solution.py:14
  444.6 11.8 %collective-permute-start.1 = (s32[128]{0:T(128)S(1)}, s32[128]{0:T(128)S(1)}, u32[]{:S(2)}, u32[]{:S(2)}) collective-permute-start(s32[128]{0:T(128)S(1)} %get-tuple-element.170), channel_id=1, source_target_pairs={{0,4},{4,8},{8,12},{12,16},{16,20},{20,24},{24,28},{28,32},{32,36}... | collective-permute-start | bytes 1544 | tf_op jit(solution)/shard_map/while/body/eval_jaxpr/ppermute | solution.py:14
  457.8 13.8 %collective-permute-start = (bf16[128,512]{1,0:T(8,128)(2,1)}, bf16[128,512]{1,0:T(8,128)(2,1)S(1)}, u32[]{:S(2)}, u32[]{:S(2)}) collective-permute-start(bf16[128,512]{1,0:T(8,128)(2,1)} %get-tuple-element.169), channel_id=1, source_target_pairs={{0,4},{4,8},{8,12},{12,16},{16,20},{20,24},{24,28},{28,32},{32,36}... | collective-permute-start | bytes 393224 | tf_op jit(solution)/shard_map/while/body/eval_jaxpr/ppermute | solution.py:14
  459.7 11.8 %collective-permute-start.1 = (s32[128]{0:T(128)S(1)}, s32[128]{0:T(128)S(1)}, u32[]{:S(2)}, u32[]{:S(2)}) collective-permute-start(s32[128]{0:T(128)S(1)} %get-tuple-element.170), channel_id=1, source_target_pairs={{0,4},{4,8},{8,12},{12,16},{16,20},{20,24},{24,28},{28,32},{32,36}... | collective-permute-start | bytes 1544 | tf_op jit(solution)/shard_map/while/body/eval_jaxpr/ppermute | solution.py:14
  472.8 13.8 %collective-permute-start = (bf16[128,512]{1,0:T(8,128)(2,1)}, bf16[128,512]{1,0:T(8,128)(2,1)S(1)}, u32[]{:S(2)}, u32[]{:S(2)}) collective-permute-start(bf16[128,512]{1,0:T(8,128)(2,1)} %get-tuple-element.169), channel_id=1, source_target_pairs={{0,4},{4,8},{8,12},{12,16},{16,20},{20,24},{24,28},{28,32},{32,36}... | collective-permute-start | bytes 393224 | tf_op jit(solution)/shard_map/while/body/eval_jaxpr/ppermute | solution.py:14
  474.8 11.8 %collective-permute-start.1 = (s32[128]{0:T(128)S(1)}, s32[128]{0:T(128)S(1)}, u32[]{:S(2)}, u32[]{:S(2)}) collective-permute-start(s32[128]{0:T(128)S(1)} %get-tuple-element.170), channel_id=1, source_target_pairs={{0,4},{4,8},{8,12},{12,16},{16,20},{20,24},{24,28},{28,32},{32,36}... | collective-permute-start | bytes 1544 | tf_op jit(solution)/shard_map/while/body/eval_jaxpr/ppermute | solution.py:14
  487.9 13.8 %collective-permute-start = (bf16[128,512]{1,0:T(8,128)(2,1)}, bf16[128,512]{1,0:T(8,128)(2,1)S(1)}, u32[]{:S(2)}, u32[]{:S(2)}) collective-permute-start(bf16[128,512]{1,0:T(8,128)(2,1)} %get-tuple-element.169), channel_id=1, source_target_pairs={{0,4},{4,8},{8,12},{12,16},{16,20},{20,24},{24,28},{28,32},{32,36}... | collective-permute-start | bytes 393224 | tf_op jit(solution)/shard_map/while/body/eval_jaxpr/ppermute | solution.py:14
  489.8 11.8 %collective-permute-start.1 = (s32[128]{0:T(128)S(1)}, s32[128]{0:T(128)S(1)}, u32[]{:S(2)}, u32[]{:S(2)}) collective-permute-start(s32[128]{0:T(128)S(1)} %get-tuple-element.170), channel_id=1, source_target_pairs={{0,4},{4,8},{8,12},{12,16},{16,20},{20,24},{24,28},{28,32},{32,36}... | collective-permute-start | bytes 1544 | tf_op jit(solution)/shard_map/while/body/eval_jaxpr/ppermute | solution.py:14
  503.0 13.8 %collective-permute-start = (bf16[128,512]{1,0:T(8,128)(2,1)}, bf16[128,512]{1,0:T(8,128)(2,1)S(1)}, u32[]{:S(2)}, u32[]{:S(2)}) collective-permute-start(bf16[128,512]{1,0:T(8,128)(2,1)} %get-tuple-element.169), channel_id=1, source_target_pairs={{0,4},{4,8},{8,12},{12,16},{16,20},{20,24},{24,28},{28,32},{32,36}... | collective-permute-start | bytes 393224 | tf_op jit(solution)/shard_map/while/body/eval_jaxpr/ppermute | solution.py:14
  504.9 11.8 %collective-permute-start.1 = (s32[128]{0:T(128)S(1)}, s32[128]{0:T(128)S(1)}, u32[]{:S(2)}, u32[]{:S(2)}) collective-permute-start(s32[128]{0:T(128)S(1)} %get-tuple-element.170), channel_id=1, source_target_pairs={{0,4},{4,8},{8,12},{12,16},{16,20},{20,24},{24,28},{28,32},{32,36}... | collective-permute-start | bytes 1544 | tf_op jit(solution)/shard_map/while/body/eval_jaxpr/ppermute | solution.py:14
  518.1 13.8 %collective-permute-start = (bf16[128,512]{1,0:T(8,128)(2,1)}, bf16[128,512]{1,0:T(8,128)(2,1)S(1)}, u32[]{:S(2)}, u32[]{:S(2)}) collective-permute-start(bf16[128,512]{1,0:T(8,128)(2,1)} %get-tuple-element.169), channel_id=1, source_target_pairs={{0,4},{4,8},{8,12},{12,16},{16,20},{20,24},{24,28},{28,32},{32,36}... | collective-permute-start | bytes 393224 | tf_op jit(solution)/shard_map/while/body/eval_jaxpr/ppermute | solution.py:14
  520.0 11.8 %collective-permute-start.1 = (s32[128]{0:T(128)S(1)}, s32[128]{0:T(128)S(1)}, u32[]{:S(2)}, u32[]{:S(2)}) collective-permute-start(s32[128]{0:T(128)S(1)} %get-tuple-element.170), channel_id=1, source_target_pairs={{0,4},{4,8},{8,12},{12,16},{16,20},{20,24},{24,28},{28,32},{32,36}... | collective-permute-start | bytes 1544 | tf_op jit(solution)/shard_map/while/body/eval_jaxpr/ppermute | solution.py:14
  533.2 13.8 %collective-permute-start = (bf16[128,512]{1,0:T(8,128)(2,1)}, bf16[128,512]{1,0:T(8,128)(2,1)S(1)}, u32[]{:S(2)}, u32[]{:S(2)}) collective-permute-start(bf16[128,512]{1,0:T(8,128)(2,1)} %get-tuple-element.169), channel_id=1, source_target_pairs={{0,4},{4,8},{8,12},{12,16},{16,20},{20,24},{24,28},{28,32},{32,36}... | collective-permute-start | bytes 393224 | tf_op jit(solution)/shard_map/while/body/eval_jaxpr/ppermute | solution.py:14
  535.1 11.8 %collective-permute-start.1 = (s32[128]{0:T(128)S(1)}, s32[128]{0:T(128)S(1)}, u32[]{:S(2)}, u32[]{:S(2)}) collective-permute-start(s32[128]{0:T(128)S(1)} %get-tuple-element.170), channel_id=1, source_target_pairs={{0,4},{4,8},{8,12},{12,16},{16,20},{20,24},{24,28},{28,32},{32,36}... | collective-permute-start | bytes 1544 | tf_op jit(solution)/shard_map/while/body/eval_jaxpr/ppermute | solution.py:14
  548.3 13.8 %collective-permute-start = (bf16[128,512]{1,0:T(8,128)(2,1)}, bf16[128,512]{1,0:T(8,128)(2,1)S(1)}, u32[]{:S(2)}, u32[]{:S(2)}) collective-permute-start(bf16[128,512]{1,0:T(8,128)(2,1)} %get-tuple-element.169), channel_id=1, source_target_pairs={{0,4},{4,8},{8,12},{12,16},{16,20},{20,24},{24,28},{28,32},{32,36}... | collective-permute-start | bytes 393224 | tf_op jit(solution)/shard_map/while/body/eval_jaxpr/ppermute | solution.py:14
  550.2 11.8 %collective-permute-start.1 = (s32[128]{0:T(128)S(1)}, s32[128]{0:T(128)S(1)}, u32[]{:S(2)}, u32[]{:S(2)}) collective-permute-start(s32[128]{0:T(128)S(1)} %get-tuple-element.170), channel_id=1, source_target_pairs={{0,4},{4,8},{8,12},{12,16},{16,20},{20,24},{24,28},{28,32},{32,36}... | collective-permute-start | bytes 1544 | tf_op jit(solution)/shard_map/while/body/eval_jaxpr/ppermute | solution.py:14
  566.2 3.1 copy-start.2
  566.2 3.1 copy-start.10
  569.2 1.1 copy-start.7
  569.3 1.6 copy-start.3
  569.3 1.6 copy-start.6
  569.3 1.6 copy-start.12
  569.3 1.6 copy-start.14
  573.4 1.7 copy-start
Sparse Core Ops, SparseCore 0:
  12.7 168.9 all-gather.4
  186.5 127.3 all-gather.6
  577.4 24.7 reduce-scatter.3
